TPU v7x, 32 devices: a whole 2x2x4 slice. The times are simulated.
32 devices in a mesh: req: 4 (over y, core), ad: 8 (over z, x).
Axes of the slice: x: 2, y: 2, z: 4, core: 2. Of those that a mesh axis runs over, the one named last changes fastest.
Arguments:
- residual: bfloat16 [256, 32, 1152], P(('req', 'ad')), may hold values from -16 to 16
- lengths: int32 [256], P(('req', 'ad')), may hold values from 1 to 32, 7168 in all
- adapter_ids: int32 [256], P(('req', 'ad')), may hold values from 0 to 31, as said below
- ffn_gain: float32 [1152], replicated, may hold values from 0.5 to 1.5
- w_gate_up: bfloat16 [2, 1152, 3072], replicated, may hold values from -0.1875 to 0.1875
- w_down: bfloat16 [3072, 1152], replicated, may hold values from -0.109375 to 0.109375
- adapter_input_first: bfloat16 [32, 32, 1152], P('ad'), may hold values from -0.1875 to 0.1875
- ad_out_b: bfloat16 [32, 2, 16, 3072], P('ad'), may hold values from -1.5 to 1.5
- ad_down_a: bfloat16 [32, 16, 3072], P('ad'), may hold values from -0.109375 to 0.109375
- adapter_down_second: bfloat16 [32, 16, 1152], P('ad'), may hold values from -1.5 to 1.5
- final_gain: float32 [1152], replicated, may hold values from 0.5 to 1.5
- head_weight: bfloat16 [1152, 32000], P(None, ('req', 'ad')), may hold values from -3 to 3
Outputs:
- layer_out: bfloat16 [256, 32, 1152], P(('req', 'ad'))
- log_probs: float32 [256, 32000], P(None, ('req', 'ad'))
Inputs may be any that keep to these rules, and one draw needn't show every extreme that they name: `adapter_ids`: the 8 requests of one device (aligned blocks of 8 requests in order) use adapters whose indices divided by 4 are all different.
All inputs are finite; a program needn't handle non-finite values. No bound on the sum of `lengths` on one device may be relied on, other than what follows from the above.
Results may differ from a plain program's by a relative error of at most 0.0076.
Values may be sent and summed in bfloat16 or wider, within the bound.
A program may use at most 128 MiB of HBM per device.

v0:
```python
import jax
import jax.numpy as jnp
from jax import lax
from jax.sharding import PartitionSpec as P

epsilon = 1e-05


def rms_scale(values, gain):
    mean_sq = jnp.mean(values * values, axis=-1, keepdims=True)
    return values * lax.rsqrt(mean_sq + epsilon) * gain


def picks_of(slot_ids, per_dev):
    return (slot_ids[..., None] == jnp.arange(per_dev, dtype=jnp.int32)).astype(jnp.float32)


def adapter_gate_up(row_block, picks, in_a, out_b):
    lowered = jnp.einsum("isd,akd->isak", row_block, in_a, preferred_element_type=jnp.float32)
    input_lowrank_state = jnp.sum(lowered * picks[..., None], axis=2).astype(jnp.bfloat16)
    spread = input_lowrank_state[:, :, None, :] * picks[..., None].astype(jnp.bfloat16)
    rank = out_b.shape[2]
    spread = spread.reshape(spread.shape[0], spread.shape[1], spread.shape[2], 2, rank)
    return jnp.einsum("isajr,ajrf->isjf", spread, out_b, preferred_element_type=jnp.float32).astype(
        jnp.bfloat16
    )


def adapter_down(hidden_block, picks, down_a, down_b):
    lowered = jnp.einsum("isf,akf->isak", hidden_block, down_a, preferred_element_type=jnp.float32)
    down_lowrank_state = jnp.sum(lowered * picks[..., None], axis=2).astype(jnp.bfloat16)
    spread = down_lowrank_state[:, :, None, :] * picks[..., None].astype(jnp.bfloat16)
    return jnp.einsum("isak,akd->isd", spread, down_b, preferred_element_type=jnp.float32).astype(
        jnp.bfloat16
    )


def base_gate_up(normalized_rows, w_gate_up):
    lead = normalized_rows.shape[:-1]
    flat = normalized_rows.reshape(-1, normalized_rows.shape[-1])
    gate = jnp.dot(flat, w_gate_up[0], preferred_element_type=jnp.float32)
    up_part = jnp.dot(flat, w_gate_up[1], preferred_element_type=jnp.float32)
    return (gate.reshape(lead + (gate.shape[-1],)), up_part.reshape(lead + (up_part.shape[-1],)))


def base_down(hidden, w_down):
    lead = hidden.shape[:-1]
    result = jnp.dot(
        hidden.reshape(-1, hidden.shape[-1]), w_down, preferred_element_type=jnp.float32
    )
    return result.reshape(lead + (result.shape[-1],))


def local(
    residual,
    lengths,
    adapter_ids,
    ffn_gain,
    w_gate_up,
    w_down,
    adapter_input_first,
    ad_out_b,
    ad_down_a,
    adapter_down_second,
    final_gain,
    head_weight,
):
    req_dev, seq_len, width = residual.shape
    groups = lax.axis_size("ad")
    per_dev = adapter_input_first.shape[0]
    positions = jnp.arange(seq_len, dtype=jnp.int32)
    valid = positions[None, :] < lengths[:, None]
    stream = residual.astype(jnp.float32)
    normalized_rows = rms_scale(stream, ffn_gain).astype(jnp.bfloat16)
    kept = jnp.where(valid[..., None], normalized_rows, jnp.zeros_like(normalized_rows))
    holder = adapter_ids // per_dev
    local_id = adapter_ids % per_dev
    placing = jnp.arange(groups, dtype=jnp.int32)[:, None] == holder[None, :]
    place_bf = placing.astype(jnp.bfloat16)
    slot_ids = jnp.sum(placing.astype(jnp.int32) * local_id[None, :], axis=1)
    slot_rows = jnp.broadcast_to(slot_ids[:, None], (groups, seq_len))

    def place(values):
        return jnp.einsum(
            "hr,rsf->hsf", place_bf, values, preferred_element_type=jnp.float32
        ).astype(jnp.bfloat16)

    def unplace(returned):
        return jnp.einsum("hr,hsf->rsf", place_bf, returned, preferred_element_type=jnp.float32)

    row_block = lax.all_to_all(place(kept), "ad", split_axis=0, concat_axis=0, tiled=True)
    row_ids = lax.all_to_all(slot_rows, "ad", split_axis=0, concat_axis=0, tiled=True)
    delta = adapter_gate_up(row_block, picks_of(row_ids, per_dev), adapter_input_first, ad_out_b)
    delta = delta.reshape(delta.shape[0], delta.shape[1], -1)
    returned_gu = lax.all_to_all(delta, "ad", split_axis=0, concat_axis=0, tiled=True)
    gate, up_part = base_gate_up(normalized_rows, w_gate_up)
    hidden_units = gate.shape[-1]
    delta_gu = unplace(returned_gu)
    hidden = (
        jax.nn.silu(gate + delta_gu[..., :hidden_units]) * (up_part + delta_gu[..., hidden_units:])
    ).astype(jnp.bfloat16)
    hidden_kept = jnp.where(valid[..., None], hidden, jnp.zeros_like(hidden))
    hidden_block = lax.all_to_all(place(hidden_kept), "ad", split_axis=0, concat_axis=0, tiled=True)
    row_ids = lax.all_to_all(slot_rows, "ad", split_axis=0, concat_axis=0, tiled=True)
    delta = adapter_down(hidden_block, picks_of(row_ids, per_dev), ad_down_a, adapter_down_second)
    returned_down = lax.all_to_all(delta, "ad", split_axis=0, concat_axis=0, tiled=True)
    mixed = stream + base_down(hidden, w_down) + unplace(returned_down)
    layer_out = jnp.where(valid[..., None], mixed, jnp.zeros_like(mixed)).astype(jnp.bfloat16)
    last_index = (lengths - 1)[:, None, None]
    last_row = jnp.take_along_axis(layer_out, last_index, axis=1)[:, 0, :].astype(jnp.float32)
    final = rms_scale(last_row, final_gain).astype(jnp.bfloat16)
    logits = jnp.dot(
        lax.all_gather(final, ("req", "ad"), axis=0, tiled=True),
        head_weight,
        preferred_element_type=jnp.float32,
    )
    local_max = jnp.max(logits, axis=1)
    highest = lax.pmax(local_max, ("req", "ad"))
    total = lax.psum(jnp.sum(jnp.exp(logits - highest[:, None]), axis=1), ("req", "ad"))
    log_probs = logits - highest[:, None] - jnp.log(total)[:, None]
    return (layer_out, log_probs)


def solution(mesh):
    in_specs = (
        P(("req", "ad"), None, None),
        P(("req", "ad")),
        P(("req", "ad")),
        P(),
        P(),
        P(),
        P("ad", None, None),
        P("ad", None, None, None),
        P("ad", None, None),
        P("ad", None, None),
        P(),
        P(None, ("req", "ad")),
    )
    out_specs = (P(("req", "ad"), None, None), P(None, ("req", "ad")))
    return jax.shard_map(local, mesh=mesh, in_specs=in_specs, out_specs=out_specs, check_vma=False)
```

profile of v0, /device:TPU:0, one launch (start us, length us, event | category | flops | bytes accessed | tf_op | source)
XLA Modules:
  0.0 355.6 jit_solution(7166750114568926179)
XLA Ops:
  0.6 0.0 copy-start
  0.6 0.8 and_select_fusion.1
  1.5 0.1 select_reduce_fusion
  1.5 0.7 broadcast_in_dim.35
  2.2 7.3 %all-to-all-start.1 = ((s32[8,1,32]{2,1,0:T(1,128)}), s32[8,1,32]{2,1,0:T(1,128)S(1)}, u32[]{:S(2)}, u32[]{:S(2)}) async-start(s32[8,1,32]{2,1,0:T(1,128)} %broadcast_in_dim.35), calls=%async_computation.1 | async-start | bytes 8192 | tf_op jit(solution)/shard_map/all_to_all | solution.py:92
  9.5 1.2 fusion.40
  10.7 0.7 iota_compare_fusion.2
  11.5 1.4 broadcast_select_fusion.1
  12.9 0.4 convolution_convert_fusion.1
  13.3 0.0 copy-start.2
  13.3 0.9 copy.48
  14.2 1.7 all-to-all-done.1
  15.9 4.3 %all-to-all-start = ((bf16[8,32,1152]{2,1,0:T(8,128)(2,1)}), bf16[8,32,1152]{2,1,0:T(8,128)(2,1)}, u32[]{:S(2)}, u32[]{:S(2)}) async-start(bf16[8,32,1152]{2,1,0:T(8,128)(2,1)} %copy.48), calls=%async_computation | async-start | bytes 1179648 | tf_op jit(solution)/shard_map/all_to_all | solution.py:91
  20.2 15.5 %all-to-all-done = bf16[8,32,1152]{2,1,0:T(8,128)(2,1)} async-done(((bf16[8,32,1152]{2,1,0:T(8,128)(2,1)}), bf16[8,32,1152]{2,1,0:T(8,128)(2,1)}, u32[]{:S(2)}, u32[]{:S(2)}) %all-to-all-start) | async-done | bytes 589856 | tf_op jit(solution)/shard_map/all_to_all | solution.py:91
  35.7 0.0 copy-done.8
  35.7 1.6 fusion.39
  37.3 0.1 copy.49
  37.4 0.0 copy-done.2
  37.4 1.0 fusion.8
  38.4 0.0 slice-start
  38.4 0.3 copy.84
  38.7 0.0 slice-start.1
  38.7 74.3 %all_to_all.27 = bf16[8,32,6144]{2,1,0:T(8,128)(2,1)S(1)} all-to-all(bf16[8,32,6144]{2,1,0:T(8,128)(2,1)S(1)} %bitcast.85), channel_id=1, replica_groups=mesh['req'=4,'ad'=8] {'ad'}, dimensions={0} | all-to-all | bytes 6291456 | tf_op jit(solution)/shard_map/all_to_all | solution.py:95
  113.0 3.5 fusion.21
  116.5 0.0 copy-start.4
  116.6 0.0 slice-start.3
  116.6 0.7 fusion.74
  117.3 0.0 slice-done
  117.3 0.3 copy-done.1
  117.6 0.5 slice-done.3
  118.1 3.9 %fusion.9 = f32[8,32,3072]{2,1,0:T(8,128)S(1)} fusion(bf16[2,1152,3072]{2,1,0:T(8,128)(2,1)S(1)} %bitcast.89, f32[8,32,3072]{2,0,1:T(8,128)S(1)} %get-tuple-element.2, bf16[8,32,1152]{2,1,0:T(8,128)(2,1)S(1)} %copy-done.1, f32[1152]{0:T(1024)S(1)} %copy-done.4, f32[8,32]{1,0:T(8,128)S(1)} %add_rsqrt_fusion), kind=kOutput, calls=%fused_computation.11 | convolution fusion | flops 1813905408 | bytes 13971456 | tf_op jit(solution)/shard_map/dot_general | solution.py:41
  122.1 5.1 %broadcast_select_fusion = (bf16[8,32,3072]{2,1,0:T(8,128)(2,1)S(1)}, bf16[8,32,3072]{2,1,0:T(8,128)(2,1)}) fusion(pred[8,32]{1,0:T(8,128)(4,1)S(1)} %iota_compare_fusion.2, f32[8,32,3072]{2,0,1:T(8,128)S(1)} %get-tuple-element.3, bf16[2,1152,3072]{2,1,0:T(8,128)(2,1)S(1)} %bitcast.89, bf16[8,32,1152]{2,1,0:T(8,128)(2,1)S(1)} %copy-done.1, ...), kind=kOutput, calls=%fused_computation.30 | convolution fusion | flops 1819410432 | bytes 17118208 | tf_op jit(solution)/shard_map/dot_general | solution.py:42
  127.2 1.2 convolution_convert_fusion
  128.4 2.0 copy.58
  130.4 4.5 %all-to-all-start.3 = ((bf16[8,32,3072]{2,1,0:T(8,128)(2,1)}), bf16[8,32,3072]{2,1,0:T(8,128)(2,1)}, u32[]{:S(2)}, u32[]{:S(2)}) async-start(bf16[8,32,3072]{2,1,0:T(8,128)(2,1)} %copy.58), calls=%async_computation.3 | async-start | bytes 3145728 | tf_op jit(solution)/shard_map/all_to_all | solution.py:103
  134.9 0.1 copy.60
  135.0 0.7 copy.63
  135.8 35.1 %all-to-all-done.3 = bf16[8,32,3072]{2,1,0:T(8,128)(2,1)} async-done(((bf16[8,32,3072]{2,1,0:T(8,128)(2,1)}), bf16[8,32,3072]{2,1,0:T(8,128)(2,1)}, u32[]{:S(2)}, u32[]{:S(2)}) %all-to-all-start.3) | async-done | bytes 1572896 | tf_op jit(solution)/shard_map/all_to_all | solution.py:103
  170.8 3.6 %fusion.36 = f32[8,32,4,16]{1,3,2,0:T(8,128)} fusion(bf16[8,32,3072]{2,1,0:T(8,128)(2,1)} %all-to-all-done.3, bf16[4,16,3072]{2,1,0:T(8,128)(2,1)} %param.20), kind=kOutput, calls=%fused_computation.27 | convolution fusion | flops 100663296 | bytes 2031616 | tf_op jit(solution)/shard_map/isf,akf->isak/dot_general | solution.py:30
  174.4 1.4 copy.73
  175.8 0.2 multiply_reduce_fusion
  176.1 0.1 copy.81
  176.2 0.1 copy.62
  176.3 0.0 copy-start.9
  176.3 1.5 fusion.32
  177.8 0.9 copy.64
  178.7 3.6 %all-to-all-start.4 = ((bf16[8,32,1152]{2,1,0:T(8,128)(2,1)}), bf16[8,32,1152]{2,1,0:T(8,128)(2,1)S(1)}, u32[]{:S(2)}, u32[]{:S(2)}) async-start(bf16[8,32,1152]{2,1,0:T(8,128)(2,1)} %copy.64), calls=%async_computation.4 | async-start | bytes 1179648 | tf_op jit(solution)/shard_map/all_to_all | solution.py:106
  182.3 16.0 %all-to-all-done.4 = bf16[8,32,1152]{2,1,0:T(8,128)(2,1)S(1)} async-done(((bf16[8,32,1152]{2,1,0:T(8,128)(2,1)}), bf16[8,32,1152]{2,1,0:T(8,128)(2,1)S(1)}, u32[]{:S(2)}, u32[]{:S(2)}) %all-to-all-start.4) | async-done | bytes 589856 | tf_op jit(solution)/shard_map/all_to_all | solution.py:106
  198.3 0.4 fusion.45
  198.7 0.0 copy-done.7
  198.7 0.0 copy-start.5
  198.7 5.9 %fusion.33 = bf16[8,32,1152]{2,1,0:T(8,128)(2,1)S(1)} fusion(bf16[8,32,3072]{2,1,0:T(8,128)(2,1)} %get-tuple-element.9, bf16[3072,1152]{1,0:T(8,128)(2,1)} %param.17, bf16[8,32,1152]{2,1,0:T(8,128)(2,1)S(1)} %copy-done.1, f32[8,32,1152]{2,0,1:T(8,128)S(1)} %fusion.45, pred[8,32]{1,0:T(8,128)(4,1)S(1)} %copy-done.7), kind=kOutput, calls=%fused_computation.23 | convolution fusion | flops 1813413888 | bytes 11010304 | tf_op jit(solution)/shard_map/dot_general | solution.py:48
  204.6 0.0 copy-start.3
  204.6 0.6 gather_fusion
  205.3 0.2 fusion.59
  205.5 0.1 fusion.61
  205.5 0.0 copy-done.3
  205.6 69.7 %all_gather.3 = bf16[256,1152]{1,0:T(8,128)(2,1)S(1)} all-gather(bf16[8,1152]{1,0:T(8,128)(2,1)S(1)} %fusion.61), channel_id=1, replica_groups=mesh['req'=4,'ad'=8] {'req','ad'}, dimensions={0}, use_global_device_ids=true | all-gather | bytes 608256 | tf_op jit(solution)/shard_map/all_gather | solution.py:113
  275.2 0.0 copy-done
  275.2 0.9 fusion.75
  276.2 36.9 %pmax.7 = f32[256]{0:T(256)S(1)} all-reduce(f32[256]{0:T(256)S(1)} %get-tuple-element.10), channel_id=1, replica_groups=mesh['req'=4,'ad'=8] {'req','ad'}, use_global_device_ids=true, to_apply=%region_6.7 | all-reduce | flops 256 | bytes 2048 | tf_op jit(solution)/shard_map/pmax | solution.py:118
  313.0 0.2 exponential_reduce_fusion
  313.3 41.3 %psum.7 = f32[256]{0:T(256)S(1)} all-reduce(f32[256]{0:T(256)S(1)} %exponential_reduce_fusion), channel_id=1, replica_groups=mesh['req'=4,'ad'=8] {'req','ad'}, use_global_device_ids=true, to_apply=%region_8.9 | all-reduce | flops 256 | bytes 2048 | tf_op jit(solution)/shard_map/psum | solution.py:119
  354.6 1.0 subtract_subtract_fusion
  (21 shorter events, 0.1 us)
Async XLA Ops:
  0.6 274.6 %copy-start = (bf16[1152,1000]{0,1:T(8,128)(2,1)S(1)}, bf16[1152,1000]{0,1:T(8,128)(2,1)}, u32[]{:S(2)}) copy-start(bf16[1152,1000]{0,1:T(8,128)(2,1)} %param.23) | copy-start | bytes 6912004
  2.2 13.6 %all-to-all-start.1 = ((s32[8,1,32]{2,1,0:T(1,128)}), s32[8,1,32]{2,1,0:T(1,128)S(1)}, u32[]{:S(2)}, u32[]{:S(2)}) async-start(s32[8,1,32]{2,1,0:T(1,128)} %broadcast_in_dim.35), calls=%async_computation.1 | async-start | bytes 8192 | tf_op jit(solution)/shard_map/all_to_all | solution.py:92
  11.5 110.6 %copy-start.6 = (pred[8,32]{1,0:T(8,128)(4,1)}, pred[8,32]{1,0:T(8,128)(4,1)S(1)}, u32[]{:S(2)}) copy-start(pred[8,32]{1,0:T(8,128)(4,1)S(1)} %iota_compare_fusion.2) | copy-start | bytes 772
  11.5 24.2 %copy-start.8 = (bf16[4,32,1152]{2,1,0:T(8,128)(2,1)S(1)}, bf16[4,32,1152]{2,1,0:T(8,128)(2,1)}, u32[]{:S(2)}) copy-start(bf16[4,32,1152]{2,1,0:T(8,128)(2,1)} %param.18) | copy-start | bytes 884740
  13.3 24.1 %copy-start.2 = (bf16[4,2,16,3072]{3,2,1,0:T(8,128)(2,1)S(1)}, bf16[4,2,16,3072]{3,2,1,0:T(8,128)(2,1)}, u32[]{:S(2)}) copy-start(bf16[4,2,16,3072]{3,2,1,0:T(8,128)(2,1)} %param.19) | copy-start | bytes 2359300
  15.9 19.8 %all-to-all-start = ((bf16[8,32,1152]{2,1,0:T(8,128)(2,1)}), bf16[8,32,1152]{2,1,0:T(8,128)(2,1)}, u32[]{:S(2)}, u32[]{:S(2)}) async-start(bf16[8,32,1152]{2,1,0:T(8,128)(2,1)} %copy.48), calls=%async_computation | async-start | bytes 1179648 | tf_op jit(solution)/shard_map/all_to_all | solution.py:91
  38.4 78.9 %slice-start = ((s8[14155776]{0:T(1024)(128)(4,1)}), s8[4194304]{0:T(1024)(128)(4,1)S(1)}, s32[]{:S(2)}) async-start(s8[14155776]{0:T(1024)(128)(4,1)} %bitcast.88), calls=%async_computation.5 | async-start | bytes 8388608
  38.7 78.6 %slice-start.1 = ((s8[14155776]{0:T(1024)(128)(4,1)}), s8[4194304]{0:T(1024)(128)(4,1)S(1)}, s32[]{:S(2)}) async-start(s8[14155776]{0:T(1024)(128)(4,1)} %bitcast.88), calls=%async_computation.6 | async-start | bytes 8388608
  113.0 4.3 %slice-start.2 = ((s8[14155776]{0:T(1024)(128)(4,1)}), s8[4194304]{0:T(1024)(128)(4,1)S(1)}, s32[]{:S(2)}) async-start(s8[14155776]{0:T(1024)(128)(4,1)} %bitcast.88), calls=%async_computation.7 | async-start | bytes 8388608
  116.5 1.1 copy-start.1
  116.5 1.1 copy-start.4
  116.6 1.6 slice-start.3
  130.4 40.4 %all-to-all-start.3 = ((bf16[8,32,3072]{2,1,0:T(8,128)(2,1)}), bf16[8,32,3072]{2,1,0:T(8,128)(2,1)}, u32[]{:S(2)}, u32[]{:S(2)}) async-start(bf16[8,32,3072]{2,1,0:T(8,128)(2,1)} %copy.58), calls=%async_computation.3 | async-start | bytes 3145728 | tf_op jit(solution)/shard_map/all_to_all | solution.py:103
  176.3 6.0 %copy-start.9 = (s32[8]{0:T(128)S(1)}, s32[8]{0:T(128)}, u32[]{:S(2)}) copy-start(s32[8]{0:T(128)} %param.13) | copy-start | bytes 100
  177.8 20.9 %copy-start.7 = (pred[8,32]{1,0:T(8,128)(4,1)S(1)}, pred[8,32]{1,0:T(8,128)(4,1)}, u32[]{:S(2)}) copy-start(pred[8,32]{1,0:T(8,128)(4,1)} %copy-done.6) | copy-start | bytes 772
  178.7 19.6 %all-to-all-start.4 = ((bf16[8,32,1152]{2,1,0:T(8,128)(2,1)}), bf16[8,32,1152]{2,1,0:T(8,128)(2,1)S(1)}, u32[]{:S(2)}, u32[]{:S(2)}) async-start(bf16[8,32,1152]{2,1,0:T(8,128)(2,1)} %copy.64), calls=%async_computation.4 | async-start | bytes 1179648 | tf_op jit(solution)/shard_map/all_to_all | solution.py:106
  198.7 6.8 %copy-start.5 = (f32[1152]{0:T(1024)S(1)}, f32[1152]{0:T(1024)}, u32[]{:S(2)}) copy-start(f32[1152]{0:T(1024)} %param.22) | copy-start | bytes 13828
  204.6 0.9 copy-start.3
where the time goes:
time: 356 us
  blocking collectives  222 us (62%)
  waiting for transfers between devices  68.2 us (19%)
  matrix products  29 us (8%)
  starting transfers between devices  19.7 us (6%)
  local copies, waits for them, and re-layouts  9.53 us (3%)
  other arithmetic  6.06 us (2%)
    all_to_all x1, blocking collectives, local(): lax.all_to_all(delta, 'ad', split_axis=0, concat_axis=0, tiled=True)  74.3 us
    all_gather x1, blocking collectives, local(): lax.all_gather(final, ('req', 'ad'), axis=0, tiled=True)  69.7 us
    psum x1, blocking collectives, local(): lax.psum(jnp.sum(jnp.exp(logits - highest[:, None]), axis=1), ('req', 'ad'))  41.3 us
    pmax x1, blocking collectives, local(): highest = lax.pmax(local_max, ('req', 'ad'))  36.9 us
    all_to_all x1, waiting for transfers between devices, local(): lax.all_to_all(place(hidden_kept), 'ad', split_axis=0, concat_axis=0, til...  35.1 us
    all_to_all x1, waiting for transfers between devices, local(): lax.all_to_all(delta, 'ad', split_axis=0, concat_axis=0, tiled=True)  16 us
    all_to_all x1, waiting for transfers between devices, local(): lax.all_to_all(place(kept), 'ad', split_axis=0, concat_axis=0, tiled=True)  15.5 us
    all_to_all x1, starting transfers between devices, local(): lax.all_to_all(slot_rows, 'ad', split_axis=0, concat_axis=0, tiled=True)  7.25 us
  transfers between devices with their start and end apart: 4, of which 4 were waited for; matrix products, arithmetic and copies ran while one was open for 2% of the time, Pallas kernels for 0%

commit v1 on v0

--- a/solution.py
+++ b/solution.py
@@ -116,7 +116,8 @@
     )
     local_max = jnp.max(logits, axis=1)
     highest = lax.pmax(local_max, ("req", "ad"))
-    total = lax.psum(jnp.sum(jnp.exp(logits - highest[:, None]), axis=1), ("req", "ad"))
+    partial = lax.psum(jnp.sum(jnp.exp(logits - highest[:, None]), axis=1), "ad")
+    total = lax.psum(partial, "req")
     log_probs = logits - highest[:, None] - jnp.log(total)[:, None]
     return (layer_out, log_probs)
 

time: 356 us -> 342 us (0.961)
  blocking collectives: 222 us -> 208 us
    psum x1 -> x2, blocking collectives: 41.3 us -> 27 us  [the longest x1 21.1 us: local(): lax.psum(jnp.sum(jnp.exp(logits - highest[:, None]), axis=1), 'ad')]
where the time goes in v1:
time: 342 us; the launch traced here: 341 us
  blocking collectives  208 us (61%)
  waiting for transfers between devices  68.2 us (20%)
  matrix products  29 us (8%)
  starting transfers between devices  19.7 us (6%)
  local copies, waits for them, and re-layouts  9.53 us (3%)
  other arithmetic  6.06 us (2%)
    all_to_all x1, blocking collectives, local(): lax.all_to_all(delta, 'ad', split_axis=0, concat_axis=0, tiled=True)  74.3 us
    all_gather x1, blocking collectives, local(): lax.all_gather(final, ('req', 'ad'), axis=0, tiled=True)  69.7 us
    pmax x1, blocking collectives, local(): highest = lax.pmax(local_max, ('req', 'ad'))  36.9 us
    all_to_all x1, waiting for transfers between devices, local(): lax.all_to_all(place(hidden_kept), 'ad', split_axis=0, concat_axis=0, til...  35.1 us
    psum x1, blocking collectives, local(): lax.psum(jnp.sum(jnp.exp(logits - highest[:, None]), axis=1), 'ad')  21.1 us
    all_to_all x1, waiting for transfers between devices, local(): lax.all_to_all(delta, 'ad', split_axis=0, concat_axis=0, tiled=True)  16 us
    all_to_all x1, waiting for transfers between devices, local(): lax.all_to_all(place(kept), 'ad', split_axis=0, concat_axis=0, tiled=True)  15.5 us
    all_to_all x1, starting transfers between devices, local(): lax.all_to_all(slot_rows, 'ad', split_axis=0, concat_axis=0, tiled=True)  7.25 us
  transfers between devices with their start and end apart: 4, of which 4 were waited for; matrix products, arithmetic and copies ran while one was open for 2% of the time, Pallas kernels for 0%

profile of v1, /device:TPU:0, one launch (start us, length us, event | category | flops | bytes accessed | tf_op | source)
XLA Modules:
  0.0 341.3 jit_solution(4384944987308630732)
XLA Ops:
  0.6 0.0 copy-start
  0.6 0.8 and_select_fusion.1
  1.5 0.1 select_reduce_fusion
  1.5 0.7 broadcast_in_dim.35
  2.2 7.3 %all-to-all-start.1 = ((s32[8,1,32]{2,1,0:T(1,128)}), s32[8,1,32]{2,1,0:T(1,128)S(1)}, u32[]{:S(2)}, u32[]{:S(2)}) async-start(s32[8,1,32]{2,1,0:T(1,128)} %broadcast_in_dim.35), calls=%async_computation.1 | async-start | bytes 8192 | tf_op jit(solution)/shard_map/all_to_all | solution.py:92
  9.5 1.2 fusion.40
  10.7 0.7 iota_compare_fusion.2
  11.5 1.4 broadcast_select_fusion.1
  12.9 0.4 convolution_convert_fusion.1
  13.3 0.0 copy-start.2
  13.3 0.9 copy.48
  14.2 1.7 all-to-all-done.1
  15.9 4.3 %all-to-all-start = ((bf16[8,32,1152]{2,1,0:T(8,128)(2,1)}), bf16[8,32,1152]{2,1,0:T(8,128)(2,1)}, u32[]{:S(2)}, u32[]{:S(2)}) async-start(bf16[8,32,1152]{2,1,0:T(8,128)(2,1)} %copy.48), calls=%async_computation | async-start | bytes 1179648 | tf_op jit(solution)/shard_map/all_to_all | solution.py:91
  20.2 15.5 %all-to-all-done = bf16[8,32,1152]{2,1,0:T(8,128)(2,1)} async-done(((bf16[8,32,1152]{2,1,0:T(8,128)(2,1)}), bf16[8,32,1152]{2,1,0:T(8,128)(2,1)}, u32[]{:S(2)}, u32[]{:S(2)}) %all-to-all-start) | async-done | bytes 589856 | tf_op jit(solution)/shard_map/all_to_all | solution.py:91
  35.7 0.0 copy-done.8
  35.7 1.6 fusion.39
  37.3 0.1 copy.49
  37.4 0.0 copy-done.2
  37.4 1.0 fusion.8
  38.4 0.0 slice-start
  38.4 0.3 copy.84
  38.7 0.0 slice-start.1
  38.7 74.3 %all_to_all.27 = bf16[8,32,6144]{2,1,0:T(8,128)(2,1)S(1)} all-to-all(bf16[8,32,6144]{2,1,0:T(8,128)(2,1)S(1)} %bitcast.85), channel_id=1, replica_groups=mesh['req'=4,'ad'=8] {'ad'}, dimensions={0} | all-to-all | bytes 6291456 | tf_op jit(solution)/shard_map/all_to_all | solution.py:95
  113.0 3.5 %fusion.21 = f32[8,32,6144]{2,0,1:T(8,128)S(1)} fusion(bf16[8,32,6144]{2,1,0:T(8,128)(2,1)S(1)} %all_to_all.27, s32[8]{0:T(128)S(1)} %get-tuple-element.6), kind=kOutput, calls=%fused_computation.16 | convolution fusion | flops 25165888 | bytes 9437216 | tf_op jit(solution)/shard_map/hr,hsf->rsf/dot_general | solution.py:89
  116.5 0.0 copy-start.4
  116.6 0.0 slice-start.3
  116.6 0.7 fusion.74
  117.3 0.3 copy-done.1
  117.6 0.5 slice-done.3
  118.1 3.9 %fusion.9 = f32[8,32,3072]{2,1,0:T(8,128)S(1)} fusion(bf16[2,1152,3072]{2,1,0:T(8,128)(2,1)S(1)} %bitcast.89, f32[8,32,3072]{2,0,1:T(8,128)S(1)} %get-tuple-element.2, bf16[8,32,1152]{2,1,0:T(8,128)(2,1)S(1)} %copy-done.1, f32[1152]{0:T(1024)S(1)} %copy-done.4, f32[8,32]{1,0:T(8,128)S(1)} %add_rsqrt_fusion), kind=kOutput, calls=%fused_computation.11 | convolution fusion | flops 1813905408 | bytes 13971456 | tf_op jit(solution)/shard_map/dot_general | solution.py:41
  122.1 5.1 %broadcast_select_fusion = (bf16[8,32,3072]{2,1,0:T(8,128)(2,1)S(1)}, bf16[8,32,3072]{2,1,0:T(8,128)(2,1)}) fusion(pred[8,32]{1,0:T(8,128)(4,1)S(1)} %iota_compare_fusion.2, f32[8,32,3072]{2,0,1:T(8,128)S(1)} %get-tuple-element.3, bf16[2,1152,3072]{2,1,0:T(8,128)(2,1)S(1)} %bitcast.89, bf16[8,32,1152]{2,1,0:T(8,128)(2,1)S(1)} %copy-done.1, ...), kind=kOutput, calls=%fused_computation.30 | convolution fusion | flops 1819410432 | bytes 17118208 | tf_op jit(solution)/shard_map/dot_general | solution.py:42
  127.2 1.2 convolution_convert_fusion
  128.4 2.0 copy.58
  130.4 4.5 %all-to-all-start.3 = ((bf16[8,32,3072]{2,1,0:T(8,128)(2,1)}), bf16[8,32,3072]{2,1,0:T(8,128)(2,1)}, u32[]{:S(2)}, u32[]{:S(2)}) async-start(bf16[8,32,3072]{2,1,0:T(8,128)(2,1)} %copy.58), calls=%async_computation.3 | async-start | bytes 3145728 | tf_op jit(solution)/shard_map/all_to_all | solution.py:103
  134.9 0.1 copy.60
  135.0 0.7 copy.63
  135.7 35.1 %all-to-all-done.3 = bf16[8,32,3072]{2,1,0:T(8,128)(2,1)} async-done(((bf16[8,32,3072]{2,1,0:T(8,128)(2,1)}), bf16[8,32,3072]{2,1,0:T(8,128)(2,1)}, u32[]{:S(2)}, u32[]{:S(2)}) %all-to-all-start.3) | async-done | bytes 1572896 | tf_op jit(solution)/shard_map/all_to_all | solution.py:103
  170.8 3.6 %fusion.36 = f32[8,32,4,16]{1,3,2,0:T(8,128)} fusion(bf16[8,32,3072]{2,1,0:T(8,128)(2,1)} %all-to-all-done.3, bf16[4,16,3072]{2,1,0:T(8,128)(2,1)} %param.20), kind=kOutput, calls=%fused_computation.27 | convolution fusion | flops 100663296 | bytes 2031616 | tf_op jit(solution)/shard_map/isf,akf->isak/dot_general | solution.py:30
  174.4 1.4 copy.73
  175.8 0.2 multiply_reduce_fusion
  176.0 0.1 copy.81
  176.2 0.1 copy.62
  176.3 0.0 copy-start.9
  176.3 1.5 fusion.32
  177.8 0.0 copy-start.7
  177.8 0.9 copy.64
  178.6 3.6 %all-to-all-start.4 = ((bf16[8,32,1152]{2,1,0:T(8,128)(2,1)}), bf16[8,32,1152]{2,1,0:T(8,128)(2,1)S(1)}, u32[]{:S(2)}, u32[]{:S(2)}) async-start(bf16[8,32,1152]{2,1,0:T(8,128)(2,1)} %copy.64), calls=%async_computation.4 | async-start | bytes 1179648 | tf_op jit(solution)/shard_map/all_to_all | solution.py:106
  182.3 16.0 %all-to-all-done.4 = bf16[8,32,1152]{2,1,0:T(8,128)(2,1)S(1)} async-done(((bf16[8,32,1152]{2,1,0:T(8,128)(2,1)}), bf16[8,32,1152]{2,1,0:T(8,128)(2,1)S(1)}, u32[]{:S(2)}, u32[]{:S(2)}) %all-to-all-start.4) | async-done | bytes 589856 | tf_op jit(solution)/shard_map/all_to_all | solution.py:106
  198.3 0.4 fusion.45
  198.7 0.0 copy-done.7
  198.7 0.0 copy-start.5
  198.7 5.9 %fusion.33 = bf16[8,32,1152]{2,1,0:T(8,128)(2,1)S(1)} fusion(bf16[8,32,3072]{2,1,0:T(8,128)(2,1)} %get-tuple-element.9, bf16[3072,1152]{1,0:T(8,128)(2,1)} %param.17, bf16[8,32,1152]{2,1,0:T(8,128)(2,1)S(1)} %copy-done.1, f32[8,32,1152]{2,0,1:T(8,128)S(1)} %fusion.45, pred[8,32]{1,0:T(8,128)(4,1)S(1)} %copy-done.7), kind=kOutput, calls=%fused_computation.23 | convolution fusion | flops 1813413888 | bytes 11010304 | tf_op jit(solution)/shard_map/dot_general | solution.py:48
  204.6 0.0 copy-start.3
  204.6 0.6 gather_fusion
  205.2 0.2 fusion.59
  205.4 0.1 fusion.61
  205.5 69.7 %all_gather.3 = bf16[256,1152]{1,0:T(8,128)(2,1)S(1)} all-gather(bf16[8,1152]{1,0:T(8,128)(2,1)S(1)} %fusion.61), channel_id=1, replica_groups=mesh['req'=4,'ad'=8] {'req','ad'}, dimensions={0}, use_global_device_ids=true | all-gather | bytes 608256 | tf_op jit(solution)/shard_map/all_gather | solution.py:113
  275.2 0.0 copy-done
  275.2 0.9 fusion.75
  276.1 36.9 %pmax.7 = f32[256]{0:T(256)S(1)} all-reduce(f32[256]{0:T(256)S(1)} %get-tuple-element.10), channel_id=1, replica_groups=mesh['req'=4,'ad'=8] {'req','ad'}, use_global_device_ids=true, to_apply=%region_6.7 | all-reduce | flops 256 | bytes 2048 | tf_op jit(solution)/shard_map/pmax | solution.py:118
  313.0 0.2 exponential_reduce_fusion
  313.2 21.1 %psum.14 = f32[256]{0:T(256)S(1)} all-reduce(f32[256]{0:T(256)S(1)} %exponential_reduce_fusion), channel_id=1, replica_groups=mesh['req'=4,'ad'=8] {'ad'}, use_global_device_ids=true, to_apply=%region_8.9 | all-reduce | flops 256 | bytes 2048 | tf_op jit(solution)/shard_map/psum | solution.py:119
  334.3 5.9 %psum.15 = f32[256]{0:T(256)S(1)} all-reduce(f32[256]{0:T(256)S(1)} %psum.14), channel_id=1, replica_groups=mesh['req'=4,'ad'=8] {'req'}, use_global_device_ids=true, to_apply=%region_9.10 | all-reduce | flops 256 | bytes 2048 | tf_op jit(solution)/shard_map/psum | solution.py:120
  340.2 1.0 subtract_subtract_fusion
  (22 shorter events, 0.1 us)
Async XLA Ops:
  0.6 274.6 %copy-start = (bf16[1152,1000]{0,1:T(8,128)(2,1)S(1)}, bf16[1152,1000]{0,1:T(8,128)(2,1)}, u32[]{:S(2)}) copy-start(bf16[1152,1000]{0,1:T(8,128)(2,1)} %param.23) | copy-start | bytes 6912004
  2.2 13.6 %all-to-all-start.1 = ((s32[8,1,32]{2,1,0:T(1,128)}), s32[8,1,32]{2,1,0:T(1,128)S(1)}, u32[]{:S(2)}, u32[]{:S(2)}) async-start(s32[8,1,32]{2,1,0:T(1,128)} %broadcast_in_dim.35), calls=%async_computation.1 | async-start | bytes 8192 | tf_op jit(solution)/shard_map/all_to_all | solution.py:92
  11.5 110.6 %copy-start.6 = (pred[8,32]{1,0:T(8,128)(4,1)}, pred[8,32]{1,0:T(8,128)(4,1)S(1)}, u32[]{:S(2)}) copy-start(pred[8,32]{1,0:T(8,128)(4,1)S(1)} %iota_compare_fusion.2) | copy-start | bytes 772
  11.5 24.2 %copy-start.8 = (bf16[4,32,1152]{2,1,0:T(8,128)(2,1)S(1)}, bf16[4,32,1152]{2,1,0:T(8,128)(2,1)}, u32[]{:S(2)}) copy-start(bf16[4,32,1152]{2,1,0:T(8,128)(2,1)} %param.18) | copy-start | bytes 884740
  13.3 24.1 %copy-start.2 = (bf16[4,2,16,3072]{3,2,1,0:T(8,128)(2,1)S(1)}, bf16[4,2,16,3072]{3,2,1,0:T(8,128)(2,1)}, u32[]{:S(2)}) copy-start(bf16[4,2,16,3072]{3,2,1,0:T(8,128)(2,1)} %param.19) | copy-start | bytes 2359300
  15.9 19.8 %all-to-all-start = ((bf16[8,32,1152]{2,1,0:T(8,128)(2,1)}), bf16[8,32,1152]{2,1,0:T(8,128)(2,1)}, u32[]{:S(2)}, u32[]{:S(2)}) async-start(bf16[8,32,1152]{2,1,0:T(8,128)(2,1)} %copy.48), calls=%async_computation | async-start | bytes 1179648 | tf_op jit(solution)/shard_map/all_to_all | solution.py:91
  38.4 78.9 %slice-start = ((s8[14155776]{0:T(1024)(128)(4,1)}), s8[4194304]{0:T(1024)(128)(4,1)S(1)}, s32[]{:S(2)}) async-start(s8[14155776]{0:T(1024)(128)(4,1)} %bitcast.88), calls=%async_computation.5 | async-start | bytes 8388608
  38.7 78.6 %slice-start.1 = ((s8[14155776]{0:T(1024)(128)(4,1)}), s8[4194304]{0:T(1024)(128)(4,1)S(1)}, s32[]{:S(2)}) async-start(s8[14155776]{0:T(1024)(128)(4,1)} %bitcast.88), calls=%async_computation.6 | async-start | bytes 8388608
  113.0 4.3 %slice-start.2 = ((s8[14155776]{0:T(1024)(128)(4,1)}), s8[4194304]{0:T(1024)(128)(4,1)S(1)}, s32[]{:S(2)}) async-start(s8[14155776]{0:T(1024)(128)(4,1)} %bitcast.88), calls=%async_computation.7 | async-start | bytes 8388608
  116.5 1.1 copy-start.1
  116.5 1.1 copy-start.4
  116.6 1.6 slice-start.3
  130.4 40.4 %all-to-all-start.3 = ((bf16[8,32,3072]{2,1,0:T(8,128)(2,1)}), bf16[8,32,3072]{2,1,0:T(8,128)(2,1)}, u32[]{:S(2)}, u32[]{:S(2)}) async-start(bf16[8,32,3072]{2,1,0:T(8,128)(2,1)} %copy.58), calls=%async_computation.3 | async-start | bytes 3145728 | tf_op jit(solution)/shard_map/all_to_all | solution.py:103
  176.3 6.0 %copy-start.9 = (s32[8]{0:T(128)S(1)}, s32[8]{0:T(128)}, u32[]{:S(2)}) copy-start(s32[8]{0:T(128)} %param.13) | copy-start | bytes 100
  177.8 20.9 %copy-start.7 = (pred[8,32]{1,0:T(8,128)(4,1)S(1)}, pred[8,32]{1,0:T(8,128)(4,1)}, u32[]{:S(2)}) copy-start(pred[8,32]{1,0:T(8,128)(4,1)} %copy-done.6) | copy-start | bytes 772
  178.6 19.6 %all-to-all-start.4 = ((bf16[8,32,1152]{2,1,0:T(8,128)(2,1)}), bf16[8,32,1152]{2,1,0:T(8,128)(2,1)S(1)}, u32[]{:S(2)}, u32[]{:S(2)}) async-start(bf16[8,32,1152]{2,1,0:T(8,128)(2,1)} %copy.64), calls=%async_computation.4 | async-start | bytes 1179648 | tf_op jit(solution)/shard_map/all_to_all | solution.py:106
  198.7 6.8 %copy-start.5 = (f32[1152]{0:T(1024)S(1)}, f32[1152]{0:T(1024)}, u32[]{:S(2)}) copy-start(f32[1152]{0:T(1024)} %param.22) | copy-start | bytes 13828
  204.6 0.9 copy-start.3
